TPU v7x, 256 devices: a whole 4x4x8 slice. The times are simulated.
256 devices in a mesh: ens: 2 (over x_lo), sx: 16 (over x_hi, y, core), sy: 8 (over z).
Axes of the slice: x: 4 (x_hi: 2, x_lo: 2; x = x_hi * 2 + x_lo), y: 4, z: 8, core: 2. Of those that a mesh axis runs over, the one named last changes fastest.
Arguments:
- snapshots: bfloat16 [4, 4, 128, 512, 512], P('ens', None, 'sx', 'sy'), may hold values from -6 to 6
- coefficients: bfloat16 [4, 256, 512], P('ens'), may hold values from -0.125 to 0.125
- modes: bfloat16 [4, 128, 512, 256], P(None, 'sx', 'sy'), may hold values from -12 to 12
Outputs:
- new_modes: bfloat16 [4, 128, 512, 256], P(None, 'sx', 'sy')
- gram: float32 [256, 256], replicated
- proj: float32 [4, 256, 512], P('ens')
All inputs are finite; a program needn't handle non-finite values.
Results may differ from a plain program's by a relative error of at most 0.005.
Values may be sent and summed in bfloat16 or wider, within the bound.
No kernel may reach another device: no remote copies, remote signals or barrier semaphores. Data moves between devices by JAX's collectives and lax.ppermute only.
A program may use at most 64 MiB of HBM per device.

v0:
```python
import math
import jax
import jax.numpy as jnp
from jax import lax
from jax.sharding import PartitionSpec as P

ETA = 0.25
LAM = 0.5
TAU = 0.4


def padded_2(array, sides, width):
    for axis, dim in sides:
        size, length = (lax.axis_size(axis), array.shape[dim])
        up = [(i, (i + 1) % size) for i in range(size - 1)]
        down = [(j, i) for i, j in up]
        last = lax.slice_in_dim(array, length - width, length, axis=dim)
        leading = lax.slice_in_dim(array, 0, width, axis=dim)
        before = lax.ppermute(last, axis, up)
        after = lax.ppermute(leading, axis, down)
        array = jnp.concatenate([before, array, after], axis=dim)
    return array


def bend(field):
    padded = padded_2(field, (("sx", 1), ("sy", 2)), 1).astype(jnp.float32)
    centre = padded[:, 1:-1, 1:-1]
    beside_all = (
        padded[:, 2:, 1:-1] + padded[:, :-2, 1:-1] + padded[:, 1:-1, 2:] + padded[:, 1:-1, :-2]
    )
    return 4.0 * centre - beside_all


def local(snapshots, coefficients, modes):
    members, levels, rows_x, rows_y, frames = snapshots.shape
    width = modes.shape[3]
    local_cells = levels * rows_x * rows_y
    total_cells = local_cells * lax.axis_size("sx") * lax.axis_size("sy")
    flat_modes = modes.reshape(local_cells, width)
    series = snapshots.reshape(members, local_cells, frames)
    bent = bend(modes).reshape(local_cells, width)
    partial_grad = jnp.zeros((local_cells, width), jnp.float32)
    for member in range(members):
        fitted = jnp.dot(flat_modes, coefficients[member], preferred_element_type=jnp.float32)
        misfit = (fitted - series[member].astype(jnp.float32)).astype(jnp.bfloat16)
        partial_grad = partial_grad + jnp.einsum(
            "ct,rt->cr", misfit, coefficients[member], preferred_element_type=jnp.float32
        )
    grad_full = lax.psum(partial_grad, "ens")
    moved = (flat_modes.astype(jnp.float32) - ETA * (grad_full + LAM * bent)).astype(jnp.bfloat16)
    moved_f = moved.astype(jnp.float32)
    squares = lax.psum(jnp.sum(moved_f * moved_f, axis=0), ("sx", "sy"))
    raw_gram = jnp.einsum("cr,cs->rs", moved, moved, preferred_element_type=jnp.float32)
    raw_proj = jnp.einsum("cr,mct->mrt", moved, series, preferred_element_type=jnp.float32)
    gram_sum, proj_sum = lax.psum((raw_gram, raw_proj), ("sx", "sy"))
    shrink = jnp.maximum(0.0, 1.0 - TAU / jnp.sqrt(squares / total_cells + 1e-06))
    new_modes = (
        (moved_f * shrink[None, :]).astype(jnp.bfloat16).reshape(levels, rows_x, rows_y, width)
    )
    gram = shrink[:, None] * gram_sum * shrink[None, :] / total_cells
    projected = shrink[None, :, None] * proj_sum / math.sqrt(total_cells)
    return (new_modes, gram, projected)


def solution(mesh):
    in_specs = (P("ens", None, "sx", "sy", None), P("ens", None, None), P(None, "sx", "sy", None))
    out_specs = (P(None, "sx", "sy", None), P(), P("ens", None, None))
    return jax.shard_map(local, mesh=mesh, in_specs=in_specs, out_specs=out_specs, check_vma=False)
```

profile of v0, /device:TPU:6, one launch (start us, length us, event | category | flops | bytes accessed | tf_op | source)
XLA Modules:
  0.0 1324.0 jit_solution(10424352402243552512)
XLA Ops:
  7.2 4.1 fusion.20
  11.3 4.2 fusion.9
  15.5 4.3 convolution_add_fusion
  19.9 0.0 all-reduce.6.cloned.1.call-start
  19.9 1.9 collective-permute-start
  21.9 7.3 collective-permute-start.1
  29.1 0.7 collective-permute-done
  29.9 0.1 constant_dynamic-update-slice_fusion.1
  30.0 1.7 collective-permute-done.1
  31.7 0.1 fusion.21
  31.7 1.3 collective-permute-start.3
  33.0 4.5 collective-permute-start.2
  37.6 1.6 collective-permute-done.2
  39.2 0.5 maximum_convert_fusion
  39.8 0.7 fusion.5
  40.5 56.4 %all-reduce.4.cloned.1.call-done = f32[2048,256]{1,0:T(8,128)} async-done(((f32[2048,256]{1,0:T(8,128)}), f32[2048,256]{1,0:T(8,128)}) %all-reduce.4.cloned.1.call-update) | async-done | bytes 2097168 | tf_op jit(solution)/shard_map/psum | solution.py:49
  96.9 2.5 fusion.2
  99.4 1.2 fusion.23
  100.6 2.2 convolution_bitcast_fusion
  102.9 329.3 %psum.29 = f32[256]{0:T(256)S(1)} all-reduce(f32[256]{0:T(256)S(1)} %get-tuple-element.5), channel_id=1, replica_groups=mesh['ens'=2,'sx'=16,'sy'=8] {'sx','sy'}, use_global_device_ids=true, to_apply=%region_2.0 | all-reduce | flops 256 | bytes 2048 | tf_op jit(solution)/shard_map/psum | solution.py:52
  432.2 1.2 fusion.3
  433.4 879.7 %all-reduce.6.cloned.1.call-done = (f32[256,256]{1,0:T(8,128)}, f32[2,256,512]{2,1,0:T(8,128)}) async-done(((f32[256,256]{1,0:T(8,128)}, f32[2,256,512]{2,1,0:T(8,128)}), (f32[256,256]{1,0:T(8,128)}, f32[2,256,512]{2,1,0:T(8,128)})) %all-reduce.6.cloned.1.call-update) | async-done | bytes 1310736 | tf_op jit(solution)/shard_map/psum | solution.py:55
  1313.1 1.8 multiply_multiply_fusion.1
  1314.8 2.3 multiply_multiply_fusion
  (12 shorter events, 0.2 us)
Async XLA Ops:
  7.2 4.1 copy-start.1
  7.2 89.8 %all-reduce.4.cloned.1.call-start = ((), (), s32[]{:S(2)}) async-start(), calls=%async_computation | async-start | bytes 4194304 | tf_op jit(solution)/shard_map/psum | solution.py:49
  19.9 1293.2 %all-reduce.6.cloned.1.call-start = ((), (), s32[]{:S(2)}) async-start(), calls=%async_computation.1 | async-start | bytes 2621440 | tf_op jit(solution)/shard_map/psum | solution.py:55
  19.9 9.9 collective-permute-start
  21.9 9.8 collective-permute-start.1
  31.7 5.9 collective-permute-start.3
  33.0 6.2 collective-permute-start.2
  96.9 3.7 copy-start
Sparse Core Ops, SparseCore 0:
  20.0 76.9 all-reduce.3
  103.0 1210.0 all-reduce.5
where the time goes:
time: 1320 us
  waiting for transfers between devices  940 us (71%)
  blocking collectives  329 us (25%)
  starting transfers between devices  15.1 us (1%)
  between operations  14.1 us (1%)
    psum x1, waiting for transfers between devices, local(): gram_sum, proj_sum = lax.psum((raw_gram, raw_proj), ('sx', 'sy'))  880 us
    psum x1, blocking collectives, local(): squares = lax.psum(jnp.sum(moved_f * moved_f, axis=0), ('sx', 'sy'))  329 us
    psum x1, waiting for transfers between devices, local(): grad_full = lax.psum(partial_grad, 'ens')  56.4 us
  transfers between devices with their start and end apart: 6, of which 5 were waited for; matrix products, arithmetic and copies ran while one was open for 0% of the time, Pallas kernels for 0%

commit v1 on v0

--- a/solution.py
+++ b/solution.py
@@ -49,7 +49,7 @@
     grad_full = lax.psum(partial_grad, "ens")
     moved = (flat_modes.astype(jnp.float32) - ETA * (grad_full + LAM * bent)).astype(jnp.bfloat16)
     moved_f = moved.astype(jnp.float32)
-    squares = lax.psum(jnp.sum(moved_f * moved_f, axis=0), ("sx", "sy"))
+    squares = lax.psum(lax.psum(jnp.sum(moved_f * moved_f, axis=0), "sx"), "sy")
     raw_gram = jnp.einsum("cr,cs->rs", moved, moved, preferred_element_type=jnp.float32)
     raw_proj = jnp.einsum("cr,mct->mrt", moved, series, preferred_element_type=jnp.float32)
     gram_sum, proj_sum = lax.psum((raw_gram, raw_proj), ("sx", "sy"))

time: 1320 us -> 1320 us (level)
  waiting for transfers between devices: 940 us -> 1220 us
  blocking collectives: 329 us -> 53.4 us
    psum x1, waiting for transfers between devices: 880 us -> 1160 us  [local(): gram_sum, proj_sum = lax.psum((raw_gram, raw_proj), ('sx', 'sy'))]
    psum x1 -> x2, blocking collectives: 329 us -> 53.4 us  [local(): squares = lax.psum(lax.psum(jnp.sum(moved_f * moved_f, axis=0), 'sx'), 'sy')]
where the time goes in v1:
time: 1320 us
  waiting for transfers between devices  1220 us (92%)
  blocking collectives  53.4 us (4%)
  starting transfers between devices  15.1 us (1%)
  between operations  14.1 us (1%)
    psum x1, waiting for transfers between devices, local(): gram_sum, proj_sum = lax.psum((raw_gram, raw_proj), ('sx', 'sy'))  1160 us
    psum x1, waiting for transfers between devices, local(): grad_full = lax.psum(partial_grad, 'ens')  56.4 us
    psum x2, blocking collectives, local(): squares = lax.psum(lax.psum(jnp.sum(moved_f * moved_f, axis=0), 'sx'), 'sy')  53.4 us
  transfers between devices with their start and end apart: 6, of which 5 were waited for; matrix products, arithmetic and copies ran while one was open for 0% of the time, Pallas kernels for 0%

profile of v1, /device:TPU:6, one launch (start us, length us, event | category | flops | bytes accessed | tf_op | source)
XLA Modules:
  0.0 1324.0 jit_solution(11030853641478194312)
XLA Ops:
  7.2 4.0 fusion.20
  11.3 4.2 fusion.9
  15.5 4.3 convolution_add_fusion
  19.9 1.9 collective-permute-start
  21.8 7.3 collective-permute-start.1
  29.1 0.7 collective-permute-done
  29.8 0.1 constant_dynamic-update-slice_fusion.1
  29.9 1.7 collective-permute-done.1
  31.6 0.1 fusion.21
  31.7 1.3 collective-permute-start.3
  33.0 4.5 collective-permute-start.2
  37.6 1.6 collective-permute-done.2
  39.2 0.5 maximum_convert_fusion
  39.7 0.7 fusion.5
  40.5 56.4 %all-reduce.4.cloned.1.call-done = f32[2048,256]{1,0:T(8,128)} async-done(((f32[2048,256]{1,0:T(8,128)}), f32[2048,256]{1,0:T(8,128)}) %all-reduce.4.cloned.1.call-update) | async-done | bytes 2097168 | tf_op jit(solution)/shard_map/psum | solution.py:49
  96.9 2.5 fusion.2
  99.4 1.2 fusion.23
  100.6 2.2 convolution_bitcast_fusion
  102.9 35.9 %psum.36 = f32[256]{0:T(256)S(1)} all-reduce(f32[256]{0:T(256)S(1)} %get-tuple-element.5), channel_id=1, replica_groups=mesh['ens'=2,'sx'=16,'sy'=8] {'sx'}, use_global_device_ids=true, to_apply=%region_2.0 | all-reduce | flops 256 | bytes 2048 | tf_op jit(solution)/shard_map/psum | solution.py:52
  138.8 17.4 %psum.37 = f32[256]{0:T(256)S(1)} all-reduce(f32[256]{0:T(256)S(1)} %psum.36), channel_id=1, replica_groups=mesh['ens'=2,'sx'=16,'sy'=8] {'sy'}, use_global_device_ids=true, to_apply=%region_3.0 | all-reduce | flops 256 | bytes 2048 | tf_op jit(solution)/shard_map/psum | solution.py:52
  156.2 1.2 fusion.3
  157.4 1155.6 %all-reduce.6.cloned.1.call-done = (f32[256,256]{1,0:T(8,128)}, f32[2,256,512]{2,1,0:T(8,128)}) async-done(((f32[256,256]{1,0:T(8,128)}, f32[2,256,512]{2,1,0:T(8,128)}), (f32[256,256]{1,0:T(8,128)}, f32[2,256,512]{2,1,0:T(8,128)})) %all-reduce.6.cloned.1.call-update) | async-done | bytes 1310736 | tf_op jit(solution)/shard_map/psum | solution.py:55
  1313.1 1.8 multiply_multiply_fusion.1
  1314.8 2.3 multiply_multiply_fusion
  (13 shorter events, 0.2 us)
Async XLA Ops:
  7.2 4.1 copy-start.1
  7.2 89.7 %all-reduce.4.cloned.1.call-start = ((), (), s32[]{:S(2)}) async-start(), calls=%async_computation | async-start | bytes 4194304 | tf_op jit(solution)/shard_map/psum | solution.py:49
  19.8 1293.2 %all-reduce.6.cloned.1.call-start = ((), (), s32[]{:S(2)}) async-start(), calls=%async_computation.1 | async-start | bytes 2621440 | tf_op jit(solution)/shard_map/psum | solution.py:55
  19.9 9.9 collective-permute-start
  21.8 9.8 collective-permute-start.1
  31.7 5.9 collective-permute-start.3
  33.0 6.2 collective-permute-start.2
  96.9 3.7 copy-start
Sparse Core Ops, SparseCore 0:
  20.0 76.9 all-reduce.3
  103.0 1210.0 all-reduce.5

commit v2 on v0

--- a/solution.py
+++ b/solution.py
@@ -52,7 +52,7 @@
     squares = lax.psum(jnp.sum(moved_f * moved_f, axis=0), ("sx", "sy"))
     raw_gram = jnp.einsum("cr,cs->rs", moved, moved, preferred_element_type=jnp.float32)
     raw_proj = jnp.einsum("cr,mct->mrt", moved, series, preferred_element_type=jnp.float32)
-    gram_sum, proj_sum = lax.psum((raw_gram, raw_proj), ("sx", "sy"))
+    gram_sum, proj_sum = lax.psum(lax.psum((raw_gram, raw_proj), "sy"), "sx")
     shrink = jnp.maximum(0.0, 1.0 - TAU / jnp.sqrt(squares / total_cells + 1e-06))
     new_modes = (
         (moved_f * shrink[None, :]).astype(jnp.bfloat16).reshape(levels, rows_x, rows_y, width)

time: 1320 us -> 519 us (0.39)
  waiting for transfers between devices: 940 us -> 139 us
    psum x1 -> x2, waiting for transfers between devices: 880 us -> 78.9 us  [local(): gram_sum, proj_sum = lax.psum(lax.psum((raw_gram, raw_proj), 'sy'), 'sx')]
  transfers between devices with their start and end apart: 6 -> 7, of which waited for: 5 -> 5; matrix products, arithmetic and copies ran while one was open for 0% -> 1% of each run, Pallas kernels for 0% -> 0%
where the time goes in v2:
time: 519 us
  blocking collectives  325 us (63%)
  waiting for transfers between devices  139 us (27%)
  starting transfers between devices  15.1 us (3%)
  between operations  13.8 us (3%)
  matrix products  12 us (2%)
  other arithmetic  9.05 us (2%)
    psum x1, blocking collectives, local(): squares = lax.psum(jnp.sum(moved_f * moved_f, axis=0), ('sx', 'sy'))  325 us
    psum x2, waiting for transfers between devices, local(): gram_sum, proj_sum = lax.psum(lax.psum((raw_gram, raw_proj), 'sy'), 'sx')  78.9 us
    psum x1, waiting for transfers between devices, local(): grad_full = lax.psum(partial_grad, 'ens')  56.4 us
  transfers between devices with their start and end apart: 7, of which 5 were waited for; matrix products, arithmetic and copies ran while one was open for 1% of the time, Pallas kernels for 0%

profile of v2, /device:TPU:6, one launch (start us, length us, event | category | flops | bytes accessed | tf_op | source)
XLA Modules:
  0.0 518.7 jit_solution(17409823254863314090)
XLA Ops:
  7.2 4.0 fusion.20
  11.3 4.2 fusion.9
  15.5 4.3 convolution_add_fusion
  19.9 1.9 collective-permute-start
  21.8 7.3 %collective-permute-start.1 = (bf16[4,1,64,256]{3,2,1,0:T(8,128)(2,1)S(1)}, bf16[4,1,64,256]{3,2,1,0:T(8,128)(2,1)S(1)}, u32[]{:S(2)}, u32[]{:S(2)}) collective-permute-start(bf16[4,1,64,256]{3,2,1,0:T(8,128)(2,1)S(1)} %get-tuple-element.13), channel_id=1, source_target_pairs={{8,0},{16,8},{24,16},{32,24},{40,32},{48,40},{56,48},{64,56},{72,6... | collective-permute-start | bytes 393224 | tf_op jit(solution)/shard_map/ppermute | solution.py:20
  29.1 0.7 collective-permute-done
  29.8 0.1 constant_dynamic-update-slice_fusion.1
  29.9 1.7 collective-permute-done.1
  31.6 0.1 fusion.21
  31.7 1.3 collective-permute-start.3
  33.0 4.5 collective-permute-start.2
  37.6 1.6 collective-permute-done.2
  39.2 0.5 maximum_convert_fusion
  39.7 0.7 fusion.5
  40.5 56.4 %all-reduce.6.cloned.1.call-done = f32[2048,256]{1,0:T(8,128)} async-done(((f32[2048,256]{1,0:T(8,128)}), f32[2048,256]{1,0:T(8,128)}) %all-reduce.6.cloned.1.call-update) | async-done | bytes 2097168 | tf_op jit(solution)/shard_map/psum | solution.py:49
  96.9 2.5 fusion.2
  99.4 1.2 fusion.23
  100.6 2.2 convolution_bitcast_fusion
  102.9 0.0 all-reduce.8.cloned.1.call-start
  102.9 78.9 %all-reduce.10.cloned.1.call-done = (f32[256,256]{1,0:T(8,128)}, f32[2,256,512]{2,1,0:T(8,128)}) async-done(((f32[256,256]{1,0:T(8,128)}, f32[2,256,512]{2,1,0:T(8,128)}), (f32[256,256]{1,0:T(8,128)}, f32[2,256,512]{2,1,0:T(8,128)})) %all-reduce.10.cloned.1.call-update) | async-done | bytes 1310736 | tf_op jit(solution)/shard_map/psum | solution.py:55
  181.9 325.0 %psum.43 = f32[256]{0:T(256)S(1)} all-reduce(f32[256]{0:T(256)S(1)} %get-tuple-element.7), channel_id=1, replica_groups=mesh['ens'=2,'sx'=16,'sy'=8] {'sx','sy'}, use_global_device_ids=true, to_apply=%region_2.0 | all-reduce | flops 256 | bytes 2048 | tf_op jit(solution)/shard_map/psum | solution.py:52
  506.9 1.2 fusion.3
  508.1 1.8 multiply_multiply_fusion.1
  509.9 2.3 multiply_multiply_fusion
  (15 shorter events, 0.2 us)
Async XLA Ops:
  7.2 4.1 copy-start.1
  7.2 89.7 %all-reduce.6.cloned.1.call-start = ((), (), s32[]{:S(2)}) async-start(), calls=%async_computation | async-start | bytes 4194304 | tf_op jit(solution)/shard_map/psum | solution.py:49
  19.8 162.0 %all-reduce.10.cloned.1.call-start = ((), (), s32[]{:S(2)}) async-start(), calls=%async_computation.2 | async-start | bytes 2621440 | tf_op jit(solution)/shard_map/psum | solution.py:55
  19.9 9.9 %collective-permute-start = (bf16[4,1,64,256]{3,2,1,0:T(8,128)(2,1)S(1)}, bf16[4,1,64,256]{3,2,1,0:T(8,128)(2,1)S(1)}, u32[]{:S(2)}, u32[]{:S(2)}) collective-permute-start(bf16[4,1,64,256]{3,2,1,0:T(8,128)(2,1)S(1)} %get-tuple-element.14), channel_id=1, source_target_pairs={{0,8},{8,16},{16,24},{24,32},{32,40},{40,48},{48,56},{56,64},{64,7... | collective-permute-start | bytes 393224 | tf_op jit(solution)/shard_map/ppermute | solution.py:19
  21.8 9.8 %collective-permute-start.1 = (bf16[4,1,64,256]{3,2,1,0:T(8,128)(2,1)S(1)}, bf16[4,1,64,256]{3,2,1,0:T(8,128)(2,1)S(1)}, u32[]{:S(2)}, u32[]{:S(2)}) collective-permute-start(bf16[4,1,64,256]{3,2,1,0:T(8,128)(2,1)S(1)} %get-tuple-element.13), channel_id=1, source_target_pairs={{8,0},{16,8},{24,16},{32,24},{40,32},{48,40},{56,48},{64,56},{72,6... | collective-permute-start | bytes 393224 | tf_op jit(solution)/shard_map/ppermute | solution.py:20
  31.7 5.9 %collective-permute-start.3 = (bf16[4,10,1,256]{3,2,1,0:T(2,128)(2,1)S(1)}, bf16[4,10,1,256]{3,2,1,0:T(2,128)(2,1)S(1)}, u32[]{:S(2)}, u32[]{:S(2)}) collective-permute-start(bf16[4,10,1,256]{3,2,1,0:T(2,128)(2,1)S(1)} %get-tuple-element.12), channel_id=1, source_target_pairs={{1,0},{2,1},{3,2},{4,3},{5,4},{6,5},{7,6},{9,8},{10,9},{11,10},{12... | collective-permute-start | bytes 61448 | tf_op jit(solution)/shard_map/ppermute | solution.py:20
  33.0 6.2 %collective-permute-start.2 = (bf16[4,10,1,256]{3,2,1,0:T(2,128)(2,1)S(1)}, bf16[4,10,1,256]{3,2,1,0:T(2,128)(2,1)S(1)}, u32[]{:S(2)}, u32[]{:S(2)}) collective-permute-start(bf16[4,10,1,256]{3,2,1,0:T(2,128)(2,1)S(1)} %get-tuple-element.11), channel_id=1, source_target_pairs={{0,1},{1,2},{2,3},{3,4},{4,5},{5,6},{6,7},{8,9},{9,10},{10,11},{11... | collective-permute-start | bytes 61448 | tf_op jit(solution)/shard_map/ppermute | solution.py:19
  96.9 3.7 copy-start
  102.9 405.2 %all-reduce.8.cloned.1.call-start = ((), (), s32[]{:S(2)}) async-start(), calls=%async_computation.1 | async-start | bytes 2621440 | tf_op jit(solution)/shard_map/psum | solution.py:55
Sparse Core Ops, SparseCore 0:
  20.0 76.9 all-reduce.5
  103.0 78.8 all-reduce.9
  184.8 145.3 all-reduce.7
